TPU v7x, 32 devices: a whole 2x2x4 slice. The times are simulated.
32 devices in a mesh: rows: 8 (over z, y), mk: 4 (over x, core).
Axes of the slice: x: 2, y: 2, z: 4, core: 2. Of those that a mesh axis runs over, the one named last changes fastest.
Arguments:
- solution_animal: float32 [6, 131072], P(None, ('rows', 'mk')), may hold values from -6 to 6
- solution_marker: float32 [6, 49152], P(None, 'mk'), may hold values from -6 to 6
- residual_animal: float32 [6, 131072], P(None, ('rows', 'mk')), may hold values from -6 to 6
- residual_marker: float32 [6, 49152], P(None, 'mk'), may hold values from -6 to 6
- direction_animal: float32 [6, 131072], P(None, ('rows', 'mk')), may hold values from -6 to 6
- direction_marker: float32 [6, 49152], P(None, 'mk'), may hold values from -6 to 6
- scaling_animal: float32 [6, 131072], P(None, ('rows', 'mk')), may hold values from 0.3 to 9, as said below
- scaling_marker: float32 [6, 49152], P(None, 'mk'), may hold values from 0.3 to 3
- previous_product: float32 [], replicated, may hold values from 943718.4 to 3932160
- genotypes: bfloat16 [3072, 49152], P('rows', 'mk'), may hold values from -0.0390625 to 0.0390625
- genetic_inverse: float32 [6, 6], replicated, may hold values from -0.28 to 4, as said below
- genomic_inverse: float32 [6, 6], replicated, may hold values from -0.28 to 4, as said below
- marker_inverse: float32 [6, 6], replicated, may hold values from -0.28 to 4, as said below
- residual_table: float32 [64, 6, 6], replicated, may hold values from -0.28 to 4, as said below
- pattern: int32 [131072], P(('rows', 'mk')), may hold values from 0 to 63
- sire_slot: int32 [131072], P(('rows', 'mk')), may hold values from 0 to 2048, as said below
- dam_slot: int32 [131072], P(('rows', 'mk')), may hold values from 0 to 2048, as said below
- genotype_row: int32 [131072], P(('rows', 'mk')), may hold values from 0 to 384, as said below
- send_list: int32 [8, 4, 8, 256], P('rows', 'mk'), may hold values from 0 to 4096, as said below
Outputs:
- next_solution_animal: float32 [6, 131072], P(None, ('rows', 'mk'))
- next_solution_marker: float32 [6, 49152], P(None, 'mk')
- next_residual_animal: float32 [6, 131072], P(None, ('rows', 'mk'))
- next_residual_marker: float32 [6, 49152], P(None, 'mk')
- reduction: float32 [], replicated
Inputs may be any that keep to these rules, and one draw needn't show every extreme that they name: `send_list`: used entries are distinct local animal indices of the owner; 4096 marks an empty slot, and empty slots only follow used ones. Every device's list to itself is full, and in every column some receiving row gets full lists from all owners. `sire_slot`: points at a used slot of the parent lists sent to the animal's device, or is 8 * 256 for an unknown sire. `dam_slot`: points at a used slot of the parent lists sent to the animal's device, or is 8 * 256 for an unknown dam. `genotype_row`: within the animals of one rows block, each value below 384 occurs exactly once; 384 marks an animal without genotypes. `scaling_animal`: Positive. `genetic_inverse`: symmetric and strictly diagonally dominant with positive diagonal. `genomic_inverse`: symmetric and strictly diagonally dominant with positive diagonal. `marker_inverse`: symmetric and strictly diagonally dominant with positive diagonal. `residual_table`: entry p is symmetric, zero in the rows and columns of traits whose bit of p is 0, and strictly diagonally dominant on the others.
All inputs are finite; a program needn't handle non-finite values.
Results may differ from a plain program's by a relative error of at most 0.00045.
Values sent between devices are 32-bit elements; how exact they have to be, the bound alone decides.
No kernel may reach another device: no remote copies, remote signals or barrier semaphores. Data moves between devices by JAX's collectives and lax.ppermute only.
A program may use at most 128 MiB of HBM per device.

v0:
```python
import jax
import jax.numpy as jnp
from jax import lax
from jax.sharding import PartitionSpec as P

precise = lax.Precision.HIGHEST


def local(
    solution_animal,
    solution_marker,
    residual_animal,
    residual_marker,
    direction_animal,
    direction_marker,
    scaling_animal,
    scaling_marker,
    previous_product,
    genotypes,
    genetic_inverse,
    genomic_inverse,
    marker_inverse,
    residual_table,
    pattern,
    sire_slot,
    dam_slot,
    genotype_row,
    send_list,
):
    traits = residual_animal.shape[0]
    animal_count = residual_animal.shape[1]
    row_count = lax.axis_size("rows")
    share_width = residual_marker.shape[1] // row_count
    share_start = lax.axis_index("rows") * share_width

    def marker_share_of(values):
        return lax.dynamic_slice_in_dim(values, share_start, share_width, 1)

    search_animal = scaling_animal * residual_animal
    search_marker = scaling_marker * residual_marker
    product_now, norm_before = lax.psum(
        (
            jnp.sum(residual_animal * search_animal)
            + jnp.sum(marker_share_of(residual_marker) * marker_share_of(search_marker)),
            jnp.sum(residual_animal * residual_animal)
            + jnp.sum(marker_share_of(residual_marker) ** 2),
        ),
        ("rows", "mk"),
    )
    conjugacy = product_now / previous_product
    new_animal = search_animal + conjugacy * direction_animal
    new_marker = search_marker + conjugacy * direction_marker
    capacity = send_list.shape[3]
    slot_total = row_count * capacity
    outgoing_index = send_list[0, 0]
    zero_column = jnp.zeros((traits, 1), jnp.float32)
    padded = jnp.concatenate([new_animal, zero_column], axis=1)
    outgoing = padded[:, outgoing_index]
    parents = lax.all_to_all(outgoing, "rows", split_axis=1, concat_axis=1, tiled=True).reshape(
        traits, slot_total
    )
    parents = jnp.concatenate([parents, zero_column], axis=1)
    known = (sire_slot < slot_total).astype(jnp.float32) + (dam_slot < slot_total).astype(
        jnp.float32
    )
    mendel = 1.0 / (1.0 - 0.25 * known)
    sampling = mendel[None, :] * (
        new_animal - 0.5 * parents[:, sire_slot] - 0.5 * parents[:, dam_slot]
    )
    backward = jnp.zeros((traits, slot_total + 1), jnp.float32)
    backward = backward.at[:, sire_slot].add(-0.5 * sampling).at[:, dam_slot].add(-0.5 * sampling)
    returned = lax.all_to_all(
        backward[:, :slot_total].reshape(traits, row_count, capacity),
        "rows",
        split_axis=1,
        concat_axis=1,
        tiled=True,
    )
    gathered_terms = (
        jnp.zeros((traits, animal_count + 1), jnp.float32)
        .at[:, outgoing_index.reshape(-1)]
        .add(returned.reshape(traits, slot_total))
    )
    pedigree = sampling + gathered_terms[:, :animal_count]
    genotyped = genotypes.shape[0]
    placed = (
        jnp.zeros((traits, genotyped + 1), jnp.float32)
        .at[:, genotype_row]
        .add(new_animal)[:, :genotyped]
    )
    predicted = lax.dot_general(
        new_marker.astype(jnp.bfloat16),
        genotypes,
        (((1,), (1,)), ((), ())),
        preferred_element_type=jnp.float32,
    )
    difference = lax.psum(placed - predicted, "mk")
    deviation = jnp.dot(genomic_inverse, difference, precision=precise)
    genomic_term = jnp.concatenate([deviation, zero_column], axis=1)[:, genotype_row]
    patterns = residual_table.shape[0]
    one_hot = (pattern[None, :] == jnp.arange(patterns, dtype=jnp.int32)[:, None]).astype(
        jnp.float32
    )
    blocks = jnp.dot(
        residual_table.reshape(patterns, traits * traits).T, one_hot, precision=precise
    ).reshape(traits, traits, animal_count)
    record_term = jnp.sum(blocks * new_animal[None, :, :], axis=1)
    image_animal = (
        jnp.dot(genetic_inverse, pedigree, precision=precise) + record_term + genomic_term
    )
    marker_terms = lax.dot_general(
        deviation.astype(jnp.bfloat16),
        genotypes,
        (((1,), (0,)), ((), ())),
        preferred_element_type=jnp.float32,
    )
    new_share = marker_share_of(new_marker)
    residual_share = marker_share_of(residual_marker)
    summed_terms = lax.psum(marker_terms, "rows")
    image_marker = jnp.dot(marker_inverse, new_marker, precision=precise) - summed_terms
    image_share = marker_share_of(image_marker)
    curvature = lax.psum(
        jnp.sum(new_animal * image_animal) + jnp.sum(new_share * image_share), ("rows", "mk")
    )
    step_size = product_now / curvature
    next_residual_animal = residual_animal - step_size * image_animal
    next_share = residual_share - step_size * image_share
    norm_after = lax.psum(
        jnp.sum(next_residual_animal * next_residual_animal) + jnp.sum(next_share * next_share),
        ("rows", "mk"),
    )
    reduction = norm_after / norm_before
    next_residual_marker = residual_marker - step_size * image_marker
    next_solution_animal = solution_animal + step_size * new_animal
    next_solution_marker = solution_marker + step_size * new_marker
    return (
        next_solution_animal,
        next_solution_marker,
        next_residual_animal,
        next_residual_marker,
        reduction,
    )


def solution(mesh):
    return jax.shard_map(
        local,
        mesh=mesh,
        in_specs=(
            P(None, ("rows", "mk")),
            P(None, "mk"),
            P(None, ("rows", "mk")),
            P(None, "mk"),
            P(None, ("rows", "mk")),
            P(None, "mk"),
            P(None, ("rows", "mk")),
            P(None, "mk"),
            P(),
            P("rows", "mk"),
            P(),
            P(),
            P(),
            P(),
            P(("rows", "mk")),
            P(("rows", "mk")),
            P(("rows", "mk")),
            P(("rows", "mk")),
            P("rows", "mk", None, None),
        ),
        out_specs=(
            P(None, ("rows", "mk")),
            P(None, "mk"),
            P(None, ("rows", "mk")),
            P(None, "mk"),
            P(),
        ),
        check_vma=False,
    )
```

profile of v0, /device:TPU:0, one launch (start us, length us, event | category | flops | bytes accessed | tf_op | source)
XLA Modules:
  0.0 350.0 jit_solution(8003247312584046191)
XLA Ops:
  7.2 1.2 mul.103
  8.4 1.4 multiply_reduce_fusion.8
  9.8 1.6 multiply_reduce_fusion.1
  12.7 42.0 %psum.42 = f32[]{:T(128)} all-reduce(f32[]{:T(128)S(6)} %add.109), channel_id=1, replica_groups=mesh['rows'=8,'mk'=4] {'rows','mk'}, use_global_device_ids=true, to_apply=%region_2.0 | all-reduce | flops 1 | bytes 8 | tf_op jit(solution)/shard_map/psum | solution.py:41
  56.0 0.9 multiply_add_fusion.3
  56.9 0.6 copy.61
  57.6 1.5 concatenate.9.clone
  59.1 7.1 %gather_fusion = f32[2048,6]{1,0:T(8,128)S(1)} fusion(f32[6,4097]{0,1:T(8,128)} %concatenate.9.clone, s32[2048]{0:T(1024)S(1)} %broadcast_clamp_fusion.3), kind=kCustom, calls=%fused_computation | custom fusion | bytes 106496 | tf_op jit(solution)/shard_map/gather | solution.py:58
  66.2 1.0 copy.46
  67.2 5.5 %all-to-all-start = ((f32[6,8,256]{2,0,1:T(8,128)}), f32[6,8,256]{2,0,1:T(8,128)S(1)}, u32[]{:S(2)}, u32[]{:S(2)}) async-start(f32[6,8,256]{2,0,1:T(8,128)} %bitcast.2), calls=%async_computation | async-start | bytes 131072 | tf_op jit(solution)/shard_map/all_to_all | solution.py:59
  72.7 0.6 copy.55
  73.4 0.6 broadcast_clamp_fusion
  74.0 28.3 %scatter_custom_fusion.3 = f32[6,385]{0,1:T(8,128)S(1)} fusion(s32[4096]{0:T(1024)S(1)} %get-tuple-element.21, f32[4096,6]{1,0:T(8,128)S(1)} %copy.55, f32[]{:T(128)} %constant.14.clone.1), kind=kCustom, calls=%fused_computation.39 | custom fusion | flops 24576 | bytes 9244 | tf_op jit(solution)/shard_map/scatter-add | solution.py:89
  102.5 6.2 %convolution_subtract_fusion = f32[6,384]{1,0:T(8,128)S(1)} fusion(f32[6,384]{1,0:T(8,128)S(1)} %copy.60, bf16[384,12288]{1,0:T(8,128)(2,1)} %param.28, f32[6,12288]{1,0:T(8,128)S(1)} %multiply_add_fusion.1), kind=kOutput, calls=%fused_computation.15 | convolution fusion | flops 56699136 | bytes 9750528 | tf_op jit(solution)/shard_map/dot_general | solution.py:91
  108.7 10.3 %psum.43 = f32[6,384]{1,0:T(8,128)S(1)} all-reduce(f32[6,384]{1,0:T(8,128)S(1)} %convolution_subtract_fusion), channel_id=1, replica_groups=mesh['rows'=8,'mk'=4] {'mk'}, use_global_device_ids=true, to_apply=%region_8.0 | all-reduce | flops 2304 | bytes 18432 | tf_op jit(solution)/shard_map/psum | solution.py:97
  119.0 0.1 convolution_bitcast_fusion.3
  119.2 5.8 %fusion.14 = f32[6,12288]{1,0:T(8,128)} fusion(bf16[384,12288]{1,0:T(8,128)(2,1)} %param.28, f32[6,384]{1,0:T(8,128)S(1)} %convolution_bitcast_fusion.3), kind=kOutput, calls=%fused_computation.55 | convolution fusion | flops 56625408 | bytes 9741312 | tf_op jit(solution)/shard_map/dot_general | solution.py:111
  125.1 0.6 compare_select_fusion.3
  125.7 0.6 compare_select_fusion.2
  126.3 0.5 convolution_bitcast_fusion.1
  126.8 0.6 subtract_divide_fusion
  127.5 0.4 copy.47
  128.0 14.1 %gather_fusion.1 = f32[4096,6]{1,0:T(8,128)} fusion(f32[6,2049]{0,1:T(8,128)S(1)} %concatenate.10, s32[4096]{0:T(1024)S(1)} %get-tuple-element.19), kind=kCustom, calls=%fused_computation.1 | custom fusion | bytes 212992 | tf_op jit(solution)/shard_map/gather | solution.py:68
  142.1 2.2 copy.48
  144.3 14.1 %gather_fusion.2 = f32[4096,6]{1,0:T(8,128)} fusion(f32[6,2049]{0,1:T(8,128)S(1)} %concatenate.10, s32[4096]{0:T(1024)S(1)} %get-tuple-element.17), kind=kCustom, calls=%fused_computation.2 | custom fusion | bytes 212992 | tf_op jit(solution)/shard_map/gather | solution.py:68
  158.4 2.2 copy.49
  160.7 2.0 copy.50
  162.7 22.9 %scatter_custom_fusion = f32[6,2049]{0,1:T(8,128)S(1)} fusion(s32[4096]{0:T(1024)} %get-tuple-element.18, f32[4096,6]{1,0:T(8,128)} %copy.50, f32[]{:T(128)} %constant.14.clone.1), kind=kCustom, calls=%fused_computation.20 | custom fusion | flops 24576 | bytes 49688 | tf_op jit(solution)/shard_map/scatter-add | solution.py:71
  185.6 23.0 %scatter_fusion = f32[6,2049]{0,1:T(8,128)S(1)} fusion(f32[6,2049]{0,1:T(8,128)S(1)} %scatter_custom_fusion, s32[4096]{0:T(1024)S(1)} %copy-done.8, f32[4096,6]{1,0:T(8,128)} %copy.50), kind=kCustom, calls=%fused_computation.5 | custom fusion | flops 24576 | bytes 311296 | tf_op jit(solution)/shard_map/scatter-add | solution.py:71
  208.7 1.0 copy.52
  209.6 5.8 %all-to-all-start.1 = ((f32[6,8,256]{2,0,1:T(8,128)}), f32[6,8,256]{2,0,1:T(8,128)S(1)}, u32[]{:S(2)}, u32[]{:S(2)}) async-start(f32[6,8,256]{2,0,1:T(8,128)} %copy.52), calls=%async_computation.1 | async-start | bytes 131072 | tf_op jit(solution)/shard_map/all_to_all | solution.py:72
  215.4 0.3 multiply_reduce_fusion
  215.7 0.1 copy.62
  215.9 12.7 %gather_fusion.3 = f32[4096,6]{1,0:T(8,128)S(1)} fusion(f32[6,385]{0,1:T(8,128)S(1)} %concatenate.11.clone, s32[4096]{0:T(1024)} %get-tuple-element.20), kind=kCustom, calls=%fused_computation.3 | custom fusion | bytes 212992 | tf_op jit(solution)/shard_map/gather | solution.py:99
  228.6 0.6 copy.58
  229.2 1.4 copy.53
  230.6 13.3 %scatter_custom_fusion.2 = f32[6,4097]{0,1:T(8,128)S(1)} fusion(s32[2048]{0:T(1024)S(1)} %bitcast.64, f32[2048,6]{1,0:T(8,128)} %copy.53, f32[]{:T(128)} %constant.14.clone.1), kind=kCustom, calls=%fused_computation.16 | custom fusion | flops 12288 | bytes 98840 | tf_op jit(solution)/shard_map/scatter-add | solution.py:82
  243.9 1.5 slice.21
  245.4 2.3 copy.59
  247.7 0.9 multiply_reduce_fusion.3
  248.6 1.5 fusion
  250.1 0.6 multiply_reduce_fusion.7
  252.0 40.4 %psum.45 = f32[]{:T(128)} all-reduce(f32[]{:T(128)S(6)} %add.123), channel_id=1, replica_groups=mesh['rows'=8,'mk'=4] {'rows','mk'}, use_global_device_ids=true, to_apply=%region_12.0 | all-reduce | flops 1 | bytes 8 | tf_op jit(solution)/shard_map/psum | solution.py:122
  293.7 0.7 multiply_reduce_fusion.5
  294.4 1.3 multiply_reduce_fusion.2
  295.7 1.0 multiply_subtract_fusion
  299.2 0.7 multiply_add_fusion.2
  299.9 40.8 %all-reduce.3 = (f32[]{:T(128)}, f32[]{:T(128)}) all-reduce(f32[]{:T(128)S(6)} %add.126, f32[]{:T(128)S(6)} %add.127), channel_id=1, replica_groups=mesh['rows'=8,'mk'=4] {'rows','mk'}, use_global_device_ids=true, to_apply=%region_15.0 | all-reduce | flops 2 | bytes 16 | tf_op jit(solution)/shard_map/psum | solution.py:128
  (55 shorter events, 0.6 us)
Async XLA Ops:
  7.2 241.4 %copy-start = (f32[6,6]{1,0:T(8,128)S(1)}, f32[6,6]{1,0:T(8,128)}, u32[]{:S(2)}) copy-start(f32[6,6]{1,0:T(8,128)} %param.31) | copy-start | bytes 436
  7.2 50.4 %copy-start.12 = (s32[1,1,8,256]{3,2,1,0:T(8,128)S(1)}, s32[1,1,8,256]{3,2,1,0:T(8,128)}, u32[]{:S(2)}) copy-start(s32[1,1,8,256]{3,2,1,0:T(8,128)} %param.37) | copy-start | bytes 24580
  59.1 14.3 %copy-start.14 = (s32[4096]{0:T(1024)S(1)}, s32[4096]{0:T(1024)}, u32[]{:S(2)}) copy-start(s32[4096]{0:T(1024)} %param.36) | copy-start | bytes 49156
  66.2 36.2 %copy-start.4 = (f32[6,12288]{1,0:T(8,128)S(1)}, f32[6,12288]{1,0:T(8,128)}, u32[]{:S(2)}) copy-start(f32[6,12288]{1,0:T(8,128)} %param.24) | copy-start | bytes 884740
  67.2 60.4 %all-to-all-start = ((f32[6,8,256]{2,0,1:T(8,128)}), f32[6,8,256]{2,0,1:T(8,128)S(1)}, u32[]{:S(2)}, u32[]{:S(2)}) async-start(f32[6,8,256]{2,0,1:T(8,128)} %bitcast.2), calls=%async_computation | async-start | bytes 131072 | tf_op jit(solution)/shard_map/all_to_all | solution.py:59
  72.7 175.9 %all-reduce.6.cloned.1.call-start = ((), (), s32[]{:S(2)}) async-start(), calls=%async_computation.2 | async-start | bytes 786432 | tf_op jit(solution)/shard_map/psum | solution.py:119
  102.5 16.5 %copy-start.17 = (f32[6,6]{1,0:T(8,128)S(1)}, f32[6,6]{1,0:T(8,128)}, u32[]{:S(2)}) copy-start(f32[6,6]{1,0:T(8,128)} %param.30) | copy-start | bytes 436
  119.2 5.8 %copy-start.5 = (f32[6,384]{1,0:T(8,128)}, f32[6,384]{1,0:T(8,128)S(1)}, u32[]{:S(2)}) copy-start(f32[6,384]{1,0:T(8,128)S(1)} %convolution_bitcast_fusion.3) | copy-start | bytes 27652
  119.2 5.9 %copy-start.10 = (s32[4096]{0:T(1024)S(1)}, s32[4096]{0:T(1024)}, u32[]{:S(2)}) copy-start(s32[4096]{0:T(1024)} %param.34) | copy-start | bytes 49156
  119.2 6.5 %copy-start.9 = (s32[4096]{0:T(1024)S(1)}, s32[4096]{0:T(1024)}, u32[]{:S(2)}) copy-start(s32[4096]{0:T(1024)} %param.35) | copy-start | bytes 49156
  119.2 7.1 %copy-start.13 = (f32[64,6,6]{0,2,1:T(8,128)S(1)}, f32[64,6,6]{0,2,1:T(8,128)}, u32[]{:S(2)}) copy-start(f32[64,6,6]{0,2,1:T(8,128)} %param.32) | copy-start | bytes 27652
  119.2 7.1 %copy-start.15 = (s32[4096]{0:T(1024)S(1)}, s32[4096]{0:T(1024)}, u32[]{:S(2)}) copy-start(s32[4096]{0:T(1024)} %param.33) | copy-start | bytes 49156
  144.3 16.3 %copy-start.11 = (f32[4096]{0:T(1024)S(1)}, f32[4096]{0:T(1024)}, u32[]{:S(2)}) copy-start(f32[4096]{0:T(1024)} %subtract_divide_fusion) | copy-start | bytes 49156
  160.6 24.9 %copy-start.8 = (s32[4096]{0:T(1024)S(1)}, s32[4096]{0:T(1024)}, u32[]{:S(2)}) copy-start(s32[4096]{0:T(1024)} %get-tuple-element.16) | copy-start | bytes 49156
  208.7 7.0 %copy-start.6 = (f32[6,384]{1,0:T(8,128)S(1)}, f32[6,384]{1,0:T(8,128)}, u32[]{:S(2)}) copy-start(f32[6,384]{1,0:T(8,128)} %copy-done.5) | copy-start | bytes 27652
  209.6 19.6 %all-to-all-start.1 = ((f32[6,8,256]{2,0,1:T(8,128)}), f32[6,8,256]{2,0,1:T(8,128)S(1)}, u32[]{:S(2)}, u32[]{:S(2)}) async-start(f32[6,8,256]{2,0,1:T(8,128)} %copy.52), calls=%async_computation.1 | async-start | bytes 131072 | tf_op jit(solution)/shard_map/all_to_all | solution.py:72
  245.4 2.3 copy-start.16
  245.4 48.3 %copy-start.1 = (f32[6,12288]{1,0:T(8,128)S(1)}, f32[6,12288]{1,0:T(8,128)}, u32[]{:S(2)}) copy-start(f32[6,12288]{1,0:T(8,128)} %param.22) | copy-start | bytes 884740
  245.4 49.0 %copy-start.2 = (f32[6,4096]{1,0:T(8,128)S(1)}, f32[6,4096]{1,0:T(8,128)}, u32[]{:S(2)}) copy-start(f32[6,4096]{1,0:T(8,128)} %param.21) | copy-start | bytes 294916
  245.4 50.3 %copy-start.3 = (f32[6,12288]{1,0:T(8,128)S(1)}, f32[6,12288]{1,0:T(8,128)}, u32[]{:S(2)}) copy-start(f32[6,12288]{1,0:T(8,128)} %param.20) | copy-start | bytes 884740
  248.6 50.6 %copy-start.7 = (f32[6,4096]{1,0:T(8,128)S(1)}, f32[6,4096]{1,0:T(8,128)}, u32[]{:S(2)}) copy-start(f32[6,4096]{1,0:T(8,128)} %param.19) | copy-start | bytes 294916
Sparse Core Ops, SparseCore 0:
  125.2 72.0 all-reduce.5
where the time goes:
time: 351 us; the launch traced here: 350 us
  blocking collectives  133 us (38%)
  other arithmetic  99.7 us (28%)
  local copies, waits for them, and re-layouts  65.8 us (19%)
  between operations  24.7 us (7%)
  matrix products  15 us (4%)
  starting transfers between devices  11.4 us (3%)
    scatter-add x2, other arithmetic, local(): backward.at[:, sire_slot].add(-0.5 * sampling).at[:, dam_slot]  45.9 us
    psum x1, blocking collectives, local(): lax.psum((jnp.sum(residual_animal * search_animal) + jnp.sum(marker_share...  42 us
    psum x1, blocking collectives, local(): lax.psum(jnp.sum(next_residual_animal * next_residual_animal) + jnp.sum(n...  40.8 us
    psum x1, blocking collectives, local(): lax.psum(jnp.sum(new_animal * image_animal) + jnp.sum(new_share * image_s...  40.4 us
    scatter-add x1, other arithmetic, local(): placed = jnp.zeros((traits, genotyped + 1), jnp.float32).at[:, genotype_r...  28.3 us
    gather x2, local copies, waits for them, and re-layouts, local(): parents[:, sire_slot]  16.3 us
    gather x2, local copies, waits for them, and re-layouts, local(): parents[:, dam_slot]  16.3 us
    gather x2, local copies, waits for them, and re-layouts, local(): jnp.concatenate([deviation, zero_column], axis=1)[:, genotype_row]  13.4 us
  transfers between devices with their start and end apart: 3, of which 0 were waited for; matrix products, arithmetic and copies ran while one was open for 46% of the time, Pallas kernels for 0%

commit v1 on v0

--- a/solution.py
+++ b/solution.py
@@ -39,13 +39,16 @@
     search_animal = scaling_animal * residual_animal
     search_marker = scaling_marker * residual_marker
     product_now, norm_before = lax.psum(
-        (
-            jnp.sum(residual_animal * search_animal)
-            + jnp.sum(marker_share_of(residual_marker) * marker_share_of(search_marker)),
-            jnp.sum(residual_animal * residual_animal)
-            + jnp.sum(marker_share_of(residual_marker) ** 2),
+        lax.psum(
+            (
+                jnp.sum(residual_animal * search_animal)
+                + jnp.sum(marker_share_of(residual_marker) * marker_share_of(search_marker)),
+                jnp.sum(residual_animal * residual_animal)
+                + jnp.sum(marker_share_of(residual_marker) ** 2),
+            ),
+            "mk",
         ),
-        ("rows", "mk"),
+        "rows",
     )
     conjugacy = product_now / previous_product
     new_animal = search_animal + conjugacy * direction_animal

time: 351 us -> 363 us (1.034)
  blocking collectives: 133 us -> 146 us
    psum x0 -> x2, blocking collectives: none -> 43.5 us  [local(): lax.psum(lax.psum((jnp.sum(residual_animal * search_animal) + jnp.sum(mar...]
    psum x1 -> x2, blocking collectives: 42 us -> 15.4 us  [local(): lax.psum((jnp.sum(residual_animal * search_animal) + jnp.sum(marker_share...]
    psum x1, blocking collectives: 40.8 us -> 36.8 us  [local(): lax.psum(jnp.sum(next_residual_animal * next_residual_animal) + jnp.sum(n...]
  transfers between devices with their start and end apart: 3 -> 3, of which waited for: 0 -> 0; matrix products, arithmetic and copies ran while one was open for 46% -> 44% of each run, Pallas kernels for 0% -> 0%
where the time goes in v1:
time: 363 us; the launch traced here: 361 us
  blocking collectives  146 us (40%)
  other arithmetic  99.6 us (27%)
  local copies, waits for them, and re-layouts  66.4 us (18%)
  between operations  24.7 us (7%)
  matrix products  15 us (4%)
  starting transfers between devices  9.17 us (3%)
    scatter-add x2, other arithmetic, local(): backward.at[:, sire_slot].add(-0.5 * sampling).at[:, dam_slot]  46.1 us
    psum x2, blocking collectives, local(): lax.psum(lax.psum((jnp.sum(residual_animal * search_animal) + jnp.sum(mar...  43.5 us
    psum x1, blocking collectives, local(): lax.psum(jnp.sum(new_animal * image_animal) + jnp.sum(new_share * image_s...  40.3 us
    psum x1, blocking collectives, local(): lax.psum(jnp.sum(next_residual_animal * next_residual_animal) + jnp.sum(n...  36.8 us
    scatter-add x1, other arithmetic, local(): placed = jnp.zeros((traits, genotyped + 1), jnp.float32).at[:, genotype_r...  28.3 us
    gather x2, local copies, waits for them, and re-layouts, local(): parents[:, sire_slot]  16.3 us
    gather x2, local copies, waits for them, and re-layouts, local(): parents[:, dam_slot]  16.3 us
    psum x2, blocking collectives, local(): lax.psum((jnp.sum(residual_animal * search_animal) + jnp.sum(marker_share...  15.4 us
  transfers between devices with their start and end apart: 3, of which 0 were waited for; matrix products, arithmetic and copies ran while one was open for 44% of the time, Pallas kernels for 0%

profile of v1, /device:TPU:0, one launch (start us, length us, event | category | flops | bytes accessed | tf_op | source)
XLA Modules:
  0.0 361.0 jit_solution(12310229893357568150)
XLA Ops:
  7.2 1.2 mul.103
  8.4 1.4 multiply_reduce_fusion.8
  9.8 1.6 multiply_reduce_fusion.1
  12.7 8.9 %psum.56 = f32[]{:T(128)} all-reduce(f32[]{:T(128)S(6)} %add.113), channel_id=1, replica_groups=mesh['rows'=8,'mk'=4] {'mk'}, use_global_device_ids=true, to_apply=%region_2.0 | all-reduce | flops 1 | bytes 8 | tf_op jit(solution)/shard_map/psum | solution.py:42
  21.6 22.3 %psum.57 = f32[]{:T(128)} all-reduce(f32[]{:T(128)} %psum.56), channel_id=1, replica_groups=mesh['rows'=8,'mk'=4] {'rows'}, use_global_device_ids=true, to_apply=%region_3.0 | all-reduce | flops 1 | bytes 8 | tf_op jit(solution)/shard_map/psum | solution.py:41
  45.2 0.9 multiply_add_fusion.3
  46.1 0.6 copy.61
  46.8 1.5 concatenate.9.clone
  48.3 7.1 %gather_fusion = f32[2048,6]{1,0:T(8,128)S(1)} fusion(f32[6,4097]{0,1:T(8,128)} %concatenate.9.clone, s32[2048]{0:T(1024)S(1)} %broadcast_clamp_fusion.3), kind=kCustom, calls=%fused_computation | custom fusion | bytes 106496 | tf_op jit(solution)/shard_map/gather | solution.py:61
  55.4 1.0 copy.46
  56.4 3.4 all-to-all-start
  59.8 0.6 copy.55
  60.4 0.6 broadcast_clamp_fusion
  61.0 28.3 %scatter_custom_fusion.3 = f32[6,385]{0,1:T(8,128)S(1)} fusion(s32[4096]{0:T(1024)S(1)} %get-tuple-element.19, f32[4096,6]{1,0:T(8,128)S(1)} %copy.55, f32[]{:T(128)} %constant.14.clone.1), kind=kCustom, calls=%fused_computation.39 | custom fusion | flops 24576 | bytes 9244 | tf_op jit(solution)/shard_map/scatter-add | solution.py:92
  89.5 6.2 %convolution_subtract_fusion = f32[6,384]{1,0:T(8,128)S(1)} fusion(f32[6,384]{1,0:T(8,128)S(1)} %copy.60, bf16[384,12288]{1,0:T(8,128)(2,1)} %param.28, f32[6,12288]{1,0:T(8,128)S(1)} %multiply_add_fusion.1), kind=kOutput, calls=%fused_computation.15 | convolution fusion | flops 56699136 | bytes 9750528 | tf_op jit(solution)/shard_map/dot_general | solution.py:94
  95.8 10.1 %psum.58 = f32[6,384]{1,0:T(8,128)S(1)} all-reduce(f32[6,384]{1,0:T(8,128)S(1)} %convolution_subtract_fusion), channel_id=1, replica_groups=mesh['rows'=8,'mk'=4] {'mk'}, use_global_device_ids=true, to_apply=%region_9.0 | all-reduce | flops 2304 | bytes 18432 | tf_op jit(solution)/shard_map/psum | solution.py:100
  106.0 0.6 copy-done.5
  106.7 5.8 %fusion.14 = f32[6,12288]{1,0:T(8,128)} fusion(bf16[384,12288]{1,0:T(8,128)(2,1)} %param.28, f32[6,384]{1,0:T(8,128)S(1)} %convolution_bitcast_fusion.3), kind=kOutput, calls=%fused_computation.55 | convolution fusion | flops 56625408 | bytes 9741312 | tf_op jit(solution)/shard_map/dot_general | solution.py:114
  112.5 0.6 compare_select_fusion.3
  113.1 0.6 compare_select_fusion.2
  113.8 0.5 convolution_bitcast_fusion.1
  114.3 0.6 subtract_divide_fusion
  115.4 14.1 %gather_fusion.1 = f32[4096,6]{1,0:T(8,128)} fusion(f32[6,2049]{0,1:T(8,128)S(1)} %concatenate.10, s32[4096]{0:T(1024)S(1)} %get-tuple-element.17), kind=kCustom, calls=%fused_computation.1 | custom fusion | bytes 212992 | tf_op jit(solution)/shard_map/gather | solution.py:71
  129.5 2.2 copy.48
  131.7 14.1 %gather_fusion.2 = f32[4096,6]{1,0:T(8,128)} fusion(f32[6,2049]{0,1:T(8,128)S(1)} %concatenate.10, s32[4096]{0:T(1024)S(1)} %get-tuple-element.15), kind=kCustom, calls=%fused_computation.2 | custom fusion | bytes 212992 | tf_op jit(solution)/shard_map/gather | solution.py:71
  145.8 2.2 copy.49
  148.1 2.0 copy.50
  150.1 22.9 %scatter_custom_fusion = f32[6,2049]{0,1:T(8,128)S(1)} fusion(s32[4096]{0:T(1024)} %get-tuple-element.16, f32[4096,6]{1,0:T(8,128)} %copy.50, f32[]{:T(128)} %constant.14.clone.1), kind=kCustom, calls=%fused_computation.20 | custom fusion | flops 24576 | bytes 49688 | tf_op jit(solution)/shard_map/scatter-add | solution.py:74
  173.0 23.2 %scatter_fusion = f32[6,2049]{0,1:T(8,128)S(1)} fusion(f32[6,2049]{0,1:T(8,128)S(1)} %scatter_custom_fusion, s32[4096]{0:T(1024)S(1)} %copy-done.8, f32[4096,6]{1,0:T(8,128)} %copy.50), kind=kCustom, calls=%fused_computation.5 | custom fusion | flops 24576 | bytes 311296 | tf_op jit(solution)/shard_map/scatter-add | solution.py:74
  196.3 1.0 copy.52
  197.2 5.8 %all-to-all-start.1 = ((f32[6,8,256]{2,0,1:T(8,128)}), f32[6,8,256]{2,0,1:T(8,128)S(1)}, u32[]{:S(2)}, u32[]{:S(2)}) async-start(f32[6,8,256]{2,0,1:T(8,128)} %copy.52), calls=%async_computation.1 | async-start | bytes 131072 | tf_op jit(solution)/shard_map/all_to_all | solution.py:75
  203.5 12.7 %gather_fusion.3 = f32[4096,6]{1,0:T(8,128)S(1)} fusion(f32[6,385]{0,1:T(8,128)S(1)} %concatenate.11.clone, s32[4096]{0:T(1024)} %get-tuple-element.18), kind=kCustom, calls=%fused_computation.3 | custom fusion | bytes 212992 | tf_op jit(solution)/shard_map/gather | solution.py:102
  216.2 0.6 copy.58
  216.8 1.4 copy.53
  218.2 13.1 %scatter_custom_fusion.2 = f32[6,4097]{0,1:T(8,128)S(1)} fusion(s32[2048]{0:T(1024)S(1)} %bitcast.64, f32[2048,6]{1,0:T(8,128)} %copy.53, f32[]{:T(128)} %constant.14.clone.1), kind=kCustom, calls=%fused_computation.16 | custom fusion | flops 12288 | bytes 98840 | tf_op jit(solution)/shard_map/scatter-add | solution.py:85
  231.3 1.5 slice.21
  232.8 2.3 copy.59
  235.1 0.9 multiply_reduce_fusion.3
  236.0 1.5 fusion
  237.5 0.6 multiply_reduce_fusion.7
  239.4 40.3 %psum.60 = f32[]{:T(128)} all-reduce(f32[]{:T(128)S(6)} %add.127), channel_id=1, replica_groups=mesh['rows'=8,'mk'=4] {'rows','mk'}, use_global_device_ids=true, to_apply=%region_13.0 | all-reduce | flops 1 | bytes 8 | tf_op jit(solution)/shard_map/psum | solution.py:125
  281.1 0.6 multiply_reduce_fusion.5
  283.0 6.5 %psum.62 = f32[]{:T(128)} all-reduce(f32[]{:T(128)S(6)} %add.131), channel_id=1, replica_groups=mesh['rows'=8,'mk'=4] {'mk'}, use_global_device_ids=true, to_apply=%region_19.0 | all-reduce | flops 1 | bytes 8 | tf_op jit(solution)/shard_map/psum | solution.py:42
  289.5 1.3 multiply_reduce_fusion.2
  292.1 21.2 %psum.63 = f32[]{:T(128)} all-reduce(f32[]{:T(128)} %psum.62), channel_id=1, replica_groups=mesh['rows'=8,'mk'=4] {'rows'}, use_global_device_ids=true, to_apply=%region_20.0 | all-reduce | flops 1 | bytes 8 | tf_op jit(solution)/shard_map/psum | solution.py:41
  313.2 36.8 %psum.61 = f32[]{:T(128)} all-reduce(f32[]{:T(128)S(6)} %add.130), channel_id=1, replica_groups=mesh['rows'=8,'mk'=4] {'rows','mk'}, use_global_device_ids=true, to_apply=%region_16.0 | all-reduce | flops 1 | bytes 8 | tf_op jit(solution)/shard_map/psum | solution.py:131
  350.0 1.0 multiply_subtract_fusion
  351.0 0.7 multiply_add_fusion.2
  (58 shorter events, 1.5 us)
Async XLA Ops:
  7.2 228.8 %copy-start = (f32[6,6]{1,0:T(8,128)S(1)}, f32[6,6]{1,0:T(8,128)}, u32[]{:S(2)}) copy-start(f32[6,6]{1,0:T(8,128)} %param.31) | copy-start | bytes 436
  7.2 39.6 %copy-start.12 = (s32[1,1,8,256]{3,2,1,0:T(8,128)S(1)}, s32[1,1,8,256]{3,2,1,0:T(8,128)}, u32[]{:S(2)}) copy-start(s32[1,1,8,256]{3,2,1,0:T(8,128)} %param.37) | copy-start | bytes 24580
  48.3 12.1 %copy-start.14 = (s32[4096]{0:T(1024)S(1)}, s32[4096]{0:T(1024)}, u32[]{:S(2)}) copy-start(s32[4096]{0:T(1024)} %param.36) | copy-start | bytes 49156
  55.4 34.1 %copy-start.4 = (f32[6,12288]{1,0:T(8,128)S(1)}, f32[6,12288]{1,0:T(8,128)}, u32[]{:S(2)}) copy-start(f32[6,12288]{1,0:T(8,128)} %param.24) | copy-start | bytes 884740
  56.4 58.6 %all-to-all-start = ((f32[6,8,256]{2,0,1:T(8,128)}), f32[6,8,256]{2,0,1:T(8,128)S(1)}, u32[]{:S(2)}, u32[]{:S(2)}) async-start(f32[6,8,256]{2,0,1:T(8,128)} %bitcast.2), calls=%async_computation | async-start | bytes 131072 | tf_op jit(solution)/shard_map/all_to_all | solution.py:62
  59.7 176.2 %all-reduce.5.cloned.1.call-start = ((), (), s32[]{:S(2)}) async-start(), calls=%async_computation.2 | async-start | bytes 786432 | tf_op jit(solution)/shard_map/psum | solution.py:122
  89.5 16.4 %copy-start.17 = (f32[6,6]{1,0:T(8,128)S(1)}, f32[6,6]{1,0:T(8,128)}, u32[]{:S(2)}) copy-start(f32[6,6]{1,0:T(8,128)} %param.30) | copy-start | bytes 436
  106.0 0.6 copy-start.5
  106.6 5.9 %copy-start.10 = (s32[4096]{0:T(1024)S(1)}, s32[4096]{0:T(1024)}, u32[]{:S(2)}) copy-start(s32[4096]{0:T(1024)} %param.34) | copy-start | bytes 49156
  106.6 6.5 %copy-start.9 = (s32[4096]{0:T(1024)S(1)}, s32[4096]{0:T(1024)}, u32[]{:S(2)}) copy-start(s32[4096]{0:T(1024)} %param.35) | copy-start | bytes 49156
  106.6 7.1 %copy-start.13 = (f32[64,6,6]{0,2,1:T(8,128)S(1)}, f32[64,6,6]{0,2,1:T(8,128)}, u32[]{:S(2)}) copy-start(f32[64,6,6]{0,2,1:T(8,128)} %param.32) | copy-start | bytes 27652
  106.6 7.1 %copy-start.15 = (s32[4096]{0:T(1024)S(1)}, s32[4096]{0:T(1024)}, u32[]{:S(2)}) copy-start(s32[4096]{0:T(1024)} %param.33) | copy-start | bytes 49156
  131.7 16.3 %copy-start.11 = (f32[4096]{0:T(1024)S(1)}, f32[4096]{0:T(1024)}, u32[]{:S(2)}) copy-start(f32[4096]{0:T(1024)} %subtract_divide_fusion) | copy-start | bytes 49156
  148.1 24.9 %copy-start.8 = (s32[4096]{0:T(1024)S(1)}, s32[4096]{0:T(1024)}, u32[]{:S(2)}) copy-start(s32[4096]{0:T(1024)} %get-tuple-element.14) | copy-start | bytes 49156
  196.3 7.0 %copy-start.6 = (f32[6,384]{1,0:T(8,128)S(1)}, f32[6,384]{1,0:T(8,128)}, u32[]{:S(2)}) copy-start(f32[6,384]{1,0:T(8,128)} %copy-done.5) | copy-start | bytes 27652
  197.2 19.6 %all-to-all-start.1 = ((f32[6,8,256]{2,0,1:T(8,128)}), f32[6,8,256]{2,0,1:T(8,128)S(1)}, u32[]{:S(2)}, u32[]{:S(2)}) async-start(f32[6,8,256]{2,0,1:T(8,128)} %copy.52), calls=%async_computation.1 | async-start | bytes 131072 | tf_op jit(solution)/shard_map/all_to_all | solution.py:75
  232.8 2.3 copy-start.16
  232.8 48.3 %copy-start.1 = (f32[6,12288]{1,0:T(8,128)S(1)}, f32[6,12288]{1,0:T(8,128)}, u32[]{:S(2)}) copy-start(f32[6,12288]{1,0:T(8,128)} %param.22) | copy-start | bytes 884740
  232.8 56.7 %copy-start.2 = (f32[6,4096]{1,0:T(8,128)S(1)}, f32[6,4096]{1,0:T(8,128)}, u32[]{:S(2)}) copy-start(f32[6,4096]{1,0:T(8,128)} %param.21) | copy-start | bytes 294916
  232.8 117.2 %copy-start.3 = (f32[6,12288]{1,0:T(8,128)S(1)}, f32[6,12288]{1,0:T(8,128)}, u32[]{:S(2)}) copy-start(f32[6,12288]{1,0:T(8,128)} %param.20) | copy-start | bytes 884740
  236.0 115.0 %copy-start.7 = (f32[6,4096]{1,0:T(8,128)S(1)}, f32[6,4096]{1,0:T(8,128)}, u32[]{:S(2)}) copy-start(f32[6,4096]{1,0:T(8,128)} %param.19) | copy-start | bytes 294916
Sparse Core Ops, SparseCore 0:
  112.6 72.0 all-reduce.4
